TPU v7x, 32 devices: a whole 2x2x4 slice. The times are simulated.
32 devices in a mesh: col: 8 (over z, x), row: 4 (over y, core).
Axes of the slice: x: 2, y: 2, z: 4, core: 2. Of those that a mesh axis runs over, the one named last changes fastest.
Arguments:
- position: float32 [128, 16384], P(None, ('col', 'row')), may hold values from -6 to 6
- momentum: float32 [128, 16384], P(None, ('col', 'row')), may hold values from -6 to 6
- row_factors: bfloat16 [16384, 16, 128], P(('col', 'row')), may hold values from -1 to 1
- col_factors: bfloat16 [16384, 16, 128], P(('col', 'row')), may hold values from -1 to 1
- tile_ranks: int32 [16, 16], replicated, may hold values from 16 to 128, as said below
- log_mean: float32 [16384], P(('col', 'row')), may hold values from -0.5 to 0.5
- counts: int32 [16384], P(('col', 'row')), may hold values from 0 to 11
- step_size: float32 [128], replicated, may hold values from 0.1 to 0.3
Outputs:
- new_position: float32 [128, 16384], P(None, ('col', 'row'))
- new_momentum: float32 [128, 16384], P(None, ('col', 'row'))
- energy_change: float32 [128], replicated
Inputs may be any that keep to these rules, and one draw needn't show every extreme that they name: `tile_ranks`: every entry is a multiple of 16; in every draw some tile has rank 16 and some tile has rank 128.
All inputs are finite; a program needn't handle non-finite values.
Results may differ from a plain program's by a relative error of at most 0.004.
Values may be sent and summed in bfloat16 or wider, within the bound.
A program may use at most 128 MiB of HBM per device.

v0:
```python
import jax
import jax.numpy as jnp
from jax import lax
from jax.sharding import PartitionSpec as P


def partner_2(value, axis, stride):
    mask = 2**stride
    pairs = [(source, source ^ mask) for source in range(lax.axis_size(axis))]
    return lax.ppermute(value, axis, pairs)


def on_device(
    position, momentum, row_factors, col_factors, tile_ranks, log_mean, counts, step_size
):
    chains = position.shape[0]
    tile_count = tile_ranks.shape[0]
    ranked = row_factors.shape[2]
    device = lax.axis_index(("col", "row"))
    own_tile = device // 2
    own_half = device % 2
    levels = jnp.arange(ranked, dtype=jnp.int32)
    col_ranks = lax.dynamic_slice_in_dim(tile_ranks, own_tile, 1, 1)[:, 0]
    row_ranks = lax.dynamic_slice_in_dim(tile_ranks, own_tile, 1, 0)[0]
    col_live = (levels[None, :] < col_ranks[:, None]).astype(jnp.float32)[:, :, None]
    row_live = (levels[None, :] < row_ranks[:, None]).astype(jnp.float32)[:, :, None]
    rate_base = counts.astype(jnp.float32)[None, :]

    def deliver(partial_value):
        halved = partial_value.reshape(2 * tile_count, ranked // 2, chains)
        arrived = lax.all_to_all(halved, ("col", "row"), split_axis=0, concat_axis=0, tiled=True)
        summed = arrived.reshape(tile_count, 2, ranked // 2, chains).astype(jnp.float32).sum(axis=1)
        summed = summed.astype(jnp.bfloat16)
        partner = partner_2(summed, "row", 0)
        lower_first = jnp.concatenate([summed, partner], axis=1)
        upper_first = jnp.concatenate([partner, summed], axis=1)
        return jnp.where(own_half == 0, lower_first, upper_first)

    def gradient(values):
        rounded = values.astype(jnp.bfloat16)
        partial_value = jnp.einsum(
            "yik,hy->ikh", col_factors, rounded, preferred_element_type=jnp.float32
        )
        partial_value = (partial_value * col_live).astype(jnp.bfloat16)
        coefficient = deliver(partial_value)
        latent_field = jnp.einsum(
            "xjk,jkh->hx", row_factors, coefficient, preferred_element_type=jnp.float32
        )
        exponent = log_mean[None, :] + latent_field
        intensity = jnp.exp(exponent)
        residual = rate_base - intensity
        adjoint = jnp.einsum(
            "xjk,hx->jkh",
            row_factors,
            residual.astype(jnp.bfloat16),
            preferred_element_type=jnp.float32,
        )
        adjoint = (adjoint * row_live).astype(jnp.bfloat16)
        returned = deliver(adjoint)
        pulled = jnp.einsum(
            "yik,ikh->hy", col_factors, returned, preferred_element_type=jnp.float32
        )
        energy = jnp.sum(intensity - rate_base * exponent + 0.5 * values * values, axis=1)
        return (values - pulled, energy)

    full_step = step_size[:, None]

    def leapfrog(section, carry):
        shifted, moment, start_energy, end_energy = carry
        forces, energy = gradient(shifted)
        weight = jnp.where(section == 1, 1.0, 0.5).astype(jnp.float32)
        moment = moment - weight * full_step * forces
        advance = jnp.where(section < 2, full_step * moment, jnp.zeros_like(moment))
        shifted = shifted + advance
        start_energy = jnp.where(section == 0, energy, start_energy)
        end_energy = jnp.where(section == 2, energy, end_energy)
        return (shifted, moment, start_energy, end_energy)

    empty = jnp.zeros((chains,), jnp.float32)
    shifted, moment, start_energy, end_energy = lax.fori_loop(
        0, 3, leapfrog, (position, momentum, empty, empty)
    )
    kinetic = 0.5 * jnp.sum(moment * moment - momentum * momentum, axis=1)
    change = lax.psum(end_energy - start_energy + kinetic, ("col", "row"))
    return (shifted, moment, change)


def solution(mesh):
    in_specs = (
        P(None, ("col", "row")),
        P(None, ("col", "row")),
        P(("col", "row"), None, None),
        P(("col", "row"), None, None),
        P(),
        P(("col", "row")),
        P(("col", "row")),
        P(),
    )
    out_specs = (P(None, ("col", "row")), P(None, ("col", "row")), P())
    return jax.shard_map(
        on_device, mesh=mesh, in_specs=in_specs, out_specs=out_specs, check_vma=False
    )
```

profile of v0, /device:TPU:0, one launch (start us, length us, event | category | flops | bytes accessed | tf_op | source)
XLA Modules:
  0.0 186.0 jit_solution(8267048132765236905)
XLA Ops:
  0.6 0.0 copy-start
  0.7 0.7 copy-done
  1.3 0.2 dynamic-slice_reduce_fusion
  1.5 2.1 %copy.23 = bf16[512,16,128]{2,0,1:T(8,128)(2,1)S(1)} copy(bf16[512,16,128]{2,1,0:T(8,128)(2,1)} %param.13) | data formatting | bytes 4194304
  3.7 0.0 copy-start.7
  3.7 0.0 copy-start.3
  3.7 0.0 copy-start.6
  3.7 0.0 copy-start.8
  3.7 0.0 copy-start.9
  3.7 4.4 %copy.24 = bf16[512,16,128]{0,2,1:T(8,128)(2,1)} copy(bf16[512,16,128]{2,1,0:T(8,128)(2,1)} %param.12) | data formatting | bytes 4194304
  8.1 0.0 copy-done.3
  8.1 0.0 copy-done.6
  8.1 0.0 copy-done.8
  8.2 0.0 copy-start.4
  8.2 138.8 %while.23 = (s32[]{:T(128)}, f32[128,512]{1,0:T(8,128)S(1)}, f32[128,512]{1,0:T(8,128)S(1)}, f32[128]{0:T(128)S(1)}, f32[128]{0:T(128)S(1)}, /*index=5*/f32[128,...) while((s32[]{:T(128)}, f32[128,512]{1,0:T(8,128)S(1)}, ...), condition=%wide.region_4.5_spmd.clone, body=%wide.region_0.4_spmd.clone.sunk | while | flops 1080828416 | bytes 28880336 | solution.py:80
  8.2 0.1 convert_bitcast_fusion.4
  8.3 0.9 fusion.47
  9.2 22.7 %all_to_all.30 = bf16[32,64,128]{2,1,0:T(8,128)(2,1)S(1)} all-to-all(bf16[32,64,128]{2,1,0:T(8,128)(2,1)S(1)} %bitcast.77), channel_id=1, replica_groups=mesh['col'=8,'row'=4] {'col','row'}, dimensions={0} | all-to-all | bytes 1048576 | tf_op jit(solution)/shard_map/while/body/eval_jaxpr/all_to_all | solution.py:31
  31.9 0.1 bitcast_reduce_fusion.4
  32.0 0.1 collective-permute-start
  32.1 0.1 convert_bitcast_fusion.5
  32.1 1.4 collective-permute-done
  33.6 0.5 fusion.48
  34.1 0.7 fusion.49
  34.8 0.3 multiply_convert_fusion.2
  35.1 18.4 %all_to_all.31 = bf16[32,64,128]{2,1,0:T(8,128)(2,1)S(1)} all-to-all(bf16[32,64,128]{2,1,0:T(8,128)(2,1)S(1)} %bitcast.76), channel_id=1, replica_groups=mesh['col'=8,'row'=4] {'col','row'}, dimensions={0} | all-to-all | bytes 1048576 | tf_op jit(solution)/shard_map/while/body/eval_jaxpr/all_to_all | solution.py:31
  53.5 0.1 bitcast_reduce_fusion.5
  53.6 0.1 collective-permute-start.1
  53.7 1.6 collective-permute-done.1
  55.4 2.0 %fusion.50 = (f32[128]{0:T(128)S(1)}, f32[128,512]{1,0:T(8,128)S(1)}, f32[128,512]{1,0:T(8,128)S(1)}) fusion(f32[128,512]{1,0:T(8,128)S(1)} %get-tuple-element.580, f32[128,512]{1,0:T(8,128)S(1)} %fusion.48, f32[512]{0:T(512)S(1)} %bitcast.80, f32[128]{0:T(128)S(1)} %bitcast.82, pred[]{:T(512)S(6)} %lt.137, f32[128,512]{1,0:T(8,128)S(1)} %get-tuple-element.581, ...), kind=kOutput, calls=%fused_computation.29.clone.1 | convolution fusion | flops 271581056 | bytes 3935746 | tf_op jit(solution)/shard_map/while/body/eval_jaxpr/yik,ikh->hy/dot_general | solution.py:60
  57.4 0.1 convert_bitcast_fusion.4
  57.4 0.9 fusion.47
  58.3 18.4 %all_to_all.30 = bf16[32,64,128]{2,1,0:T(8,128)(2,1)S(1)} all-to-all(bf16[32,64,128]{2,1,0:T(8,128)(2,1)S(1)} %bitcast.77), channel_id=1, replica_groups=mesh['col'=8,'row'=4] {'col','row'}, dimensions={0} | all-to-all | bytes 1048576 | tf_op jit(solution)/shard_map/while/body/eval_jaxpr/all_to_all | solution.py:31
  76.7 0.1 bitcast_reduce_fusion.4
  76.8 0.1 collective-permute-start
  76.9 0.1 convert_bitcast_fusion.5
  77.0 1.4 collective-permute-done
  78.4 0.5 fusion.48
  78.9 0.7 fusion.49
  79.6 0.3 multiply_convert_fusion.2
  80.0 18.4 %all_to_all.31 = bf16[32,64,128]{2,1,0:T(8,128)(2,1)S(1)} all-to-all(bf16[32,64,128]{2,1,0:T(8,128)(2,1)S(1)} %bitcast.76), channel_id=1, replica_groups=mesh['col'=8,'row'=4] {'col','row'}, dimensions={0} | all-to-all | bytes 1048576 | tf_op jit(solution)/shard_map/while/body/eval_jaxpr/all_to_all | solution.py:31
  98.4 0.1 bitcast_reduce_fusion.5
  98.4 0.1 collective-permute-start.1
  98.5 1.6 collective-permute-done.1
  100.2 1.9 %fusion.50 = (f32[128]{0:T(128)S(1)}, f32[128,512]{1,0:T(8,128)S(1)}, f32[128,512]{1,0:T(8,128)S(1)}) fusion(f32[128,512]{1,0:T(8,128)S(1)} %get-tuple-element.580, f32[128,512]{1,0:T(8,128)S(1)} %fusion.48, f32[512]{0:T(512)S(1)} %bitcast.80, f32[128]{0:T(128)S(1)} %bitcast.82, pred[]{:T(512)S(6)} %lt.137, f32[128,512]{1,0:T(8,128)S(1)} %get-tuple-element.581, ...), kind=kOutput, calls=%fused_computation.29.clone.1 | convolution fusion | flops 271581056 | bytes 3935746 | tf_op jit(solution)/shard_map/while/body/eval_jaxpr/yik,ikh->hy/dot_general | solution.py:60
  102.2 0.1 convert_bitcast_fusion.4
  102.2 0.9 fusion.47
  103.2 18.4 %all_to_all.30 = bf16[32,64,128]{2,1,0:T(8,128)(2,1)S(1)} all-to-all(bf16[32,64,128]{2,1,0:T(8,128)(2,1)S(1)} %bitcast.77), channel_id=1, replica_groups=mesh['col'=8,'row'=4] {'col','row'}, dimensions={0} | all-to-all | bytes 1048576 | tf_op jit(solution)/shard_map/while/body/eval_jaxpr/all_to_all | solution.py:31
  121.6 0.1 bitcast_reduce_fusion.4
  121.6 0.1 collective-permute-start
  121.7 0.1 convert_bitcast_fusion.5
  121.8 1.4 collective-permute-done
  123.2 0.5 fusion.48
  123.7 0.7 fusion.49
  124.4 0.3 multiply_convert_fusion.2
  124.8 18.4 %all_to_all.31 = bf16[32,64,128]{2,1,0:T(8,128)(2,1)S(1)} all-to-all(bf16[32,64,128]{2,1,0:T(8,128)(2,1)S(1)} %bitcast.76), channel_id=1, replica_groups=mesh['col'=8,'row'=4] {'col','row'}, dimensions={0} | all-to-all | bytes 1048576 | tf_op jit(solution)/shard_map/while/body/eval_jaxpr/all_to_all | solution.py:31
  143.2 0.1 bitcast_reduce_fusion.5
  143.3 0.1 collective-permute-start.1
  143.4 1.6 collective-permute-done.1
  145.0 2.0 %fusion.50 = (f32[128]{0:T(128)S(1)}, f32[128,512]{1,0:T(8,128)S(1)}, f32[128,512]{1,0:T(8,128)S(1)}) fusion(f32[128,512]{1,0:T(8,128)S(1)} %get-tuple-element.580, f32[128,512]{1,0:T(8,128)S(1)} %fusion.48, f32[512]{0:T(512)S(1)} %bitcast.80, f32[128]{0:T(128)S(1)} %bitcast.82, pred[]{:T(512)S(6)} %lt.137, f32[128,512]{1,0:T(8,128)S(1)} %get-tuple-element.581, ...), kind=kOutput, calls=%fused_computation.29.clone.1 | convolution fusion | flops 271581056 | bytes 3935746 | tf_op jit(solution)/shard_map/while/body/eval_jaxpr/yik,ikh->hy/dot_general | solution.py:60
  147.0 0.0 copy-start.2
  147.0 0.0 copy-start.5
  147.0 0.1 subtract_reduce_fusion
  147.1 38.9 %psum.7 = f32[128]{0:T(128)} all-reduce(f32[128]{0:T(128)S(1)} %multiply_add_fusion), channel_id=1, replica_groups=mesh['col'=8,'row'=4] {'col','row'}, use_global_device_ids=true, to_apply=%region_6.7 | all-reduce | flops 128 | bytes 1024 | tf_op jit(solution)/shard_map/psum | solution.py:84
  (22 shorter events, 0.1 us)
Async XLA Ops:
  0.6 0.7 copy-start
  3.7 4.4 %copy-start.7 = (s32[512]{0:T(512)S(1)}, s32[512]{0:T(512)}, u32[]{:S(2)}) copy-start(s32[512]{0:T(512)} %param.16) | copy-start | bytes 6148
  3.7 4.4 %copy-start.3 = (f32[128,512]{1,0:T(8,128)S(1)}, f32[128,512]{1,0:T(8,128)}, u32[]{:S(2)}) copy-start(f32[128,512]{1,0:T(8,128)} %param.10) | copy-start | bytes 786436
  3.7 4.4 %copy-start.6 = (f32[128,512]{1,0:T(8,128)S(1)}, f32[128,512]{1,0:T(8,128)}, u32[]{:S(2)}) copy-start(f32[128,512]{1,0:T(8,128)} %param.11) | copy-start | bytes 786436
  3.7 4.4 %copy-start.8 = (f32[512]{0:T(512)S(1)}, f32[512]{0:T(512)}, u32[]{:S(2)}) copy-start(f32[512]{0:T(512)} %param.15) | copy-start | bytes 6148
  3.7 4.4 %copy-start.9 = (f32[128]{0:T(128)S(1)}, f32[128]{0:T(128)}, u32[]{:S(2)}) copy-start(f32[128]{0:T(128)} %param.17) | copy-start | bytes 1540
  8.2 138.9 %copy-start.4 = (f32[128,512]{1,0:T(8,128)S(1)}, f32[128,512]{1,0:T(8,128)}, u32[]{:S(2)}) copy-start(f32[128,512]{1,0:T(8,128)} %param.11) | copy-start | bytes 786436
  8.3 25.4 %copy-start.1 = (bf16[512,16,128]{0,2,1:T(8,128)(2,1)S(1)}, bf16[512,16,128]{0,2,1:T(8,128)(2,1)}, u32[]{:S(2)}) copy-start(bf16[512,16,128]{0,2,1:T(8,128)(2,1)} %get-tuple-element.607) | copy-start | bytes 6291460 | tf_op jit(solution)/shard_map/while
  32.0 1.6 collective-permute-start
  53.6 1.7 collective-permute-start.1
  57.4 21.0 %copy-start.1 = (bf16[512,16,128]{0,2,1:T(8,128)(2,1)S(1)}, bf16[512,16,128]{0,2,1:T(8,128)(2,1)}, u32[]{:S(2)}) copy-start(bf16[512,16,128]{0,2,1:T(8,128)(2,1)} %get-tuple-element.607) | copy-start | bytes 6291460 | tf_op jit(solution)/shard_map/while
  76.8 1.6 collective-permute-start
  98.4 1.7 collective-permute-start.1
  102.2 21.0 %copy-start.1 = (bf16[512,16,128]{0,2,1:T(8,128)(2,1)S(1)}, bf16[512,16,128]{0,2,1:T(8,128)(2,1)}, u32[]{:S(2)}) copy-start(bf16[512,16,128]{0,2,1:T(8,128)(2,1)} %get-tuple-element.607) | copy-start | bytes 6291460 | tf_op jit(solution)/shard_map/while
  121.6 1.6 collective-permute-start
  143.3 1.7 collective-permute-start.1
  147.0 39.1 %copy-start.2 = (f32[128,512]{1,0:T(8,128)}, f32[128,512]{1,0:T(8,128)S(1)}, u32[]{:S(2)}) copy-start(f32[128,512]{1,0:T(8,128)S(1)} %get-tuple-element.347) | copy-start | bytes 786436
  147.0 39.0 %copy-start.5 = (f32[128,512]{1,0:T(8,128)}, f32[128,512]{1,0:T(8,128)S(1)}, u32[]{:S(2)}) copy-start(f32[128,512]{1,0:T(8,128)S(1)} %get-tuple-element.348) | copy-start | bytes 786436
where the time goes:
time: 187 us; the launch traced here: 186 us
  blocking collectives  154 us (82%)
  matrix products  12.1 us (6%)
  waiting for transfers between devices  9.24 us (5%)
  local copies, waits for them, and re-layouts  7.44 us (4%)
  other arithmetic  2.09 us (1%)
    all_to_all x6, blocking collectives, deliver(): lax.all_to_all(halved, ('col', 'row'), split_axis=0, concat_axis=0, tiled...  115 us
    psum x1, blocking collectives, on_device(): change = lax.psum(end_energy - start_energy + kinetic, ('col', 'row'))  38.9 us
    ppermute x6, waiting for transfers between devices, partner_2(): return lax.ppermute(value, axis, pairs)  9.24 us
    unnamed x20, local copies, waits for them, and re-layouts  7.24 us
    dot_general x3, matrix products, gradient(): jnp.einsum('yik,ikh->hy', col_factors, returned, preferred_element_type=j...  5.85 us
  transfers between devices with their start and end apart: 6, of which 6 were waited for; matrix products, arithmetic and copies ran while one was open for 0% of the time, Pallas kernels for 0%

commit v1 on v0

--- a/solution.py
+++ b/solution.py
@@ -81,7 +81,7 @@
         0, 3, leapfrog, (position, momentum, empty, empty)
     )
     kinetic = 0.5 * jnp.sum(moment * moment - momentum * momentum, axis=1)
-    change = lax.psum(end_energy - start_energy + kinetic, ("col", "row"))
+    change = lax.psum(lax.psum(end_energy - start_energy + kinetic, "col"), "row")
     return (shifted, moment, change)
 
 

time: 187 us -> 173 us (0.925)
  blocking collectives: 154 us -> 140 us
    psum x1 -> x2, blocking collectives: 38.9 us -> 25 us  [the longest x1 18.8 us: on_device(): lax.psum(end_energy - start_energy + kinetic, 'col')]
where the time goes in v1:
time: 173 us; the launch traced here: 172 us
  blocking collectives  140 us (81%)
  matrix products  12.1 us (7%)
  waiting for transfers between devices  9.24 us (5%)
  local copies, waits for them, and re-layouts  7.44 us (4%)
  other arithmetic  2.09 us (1%)
    all_to_all x6, blocking collectives, deliver(): lax.all_to_all(halved, ('col', 'row'), split_axis=0, concat_axis=0, tiled...  115 us
    psum x1, blocking collectives, on_device(): lax.psum(end_energy - start_energy + kinetic, 'col')  18.8 us
    ppermute x6, waiting for transfers between devices, partner_2(): return lax.ppermute(value, axis, pairs)  9.24 us
    unnamed x20, local copies, waits for them, and re-layouts  7.24 us
    psum x1, blocking collectives, on_device(): lax.psum(lax.psum(end_energy - start_energy + kinetic, 'col'), 'row')  6.15 us
    dot_general x3, matrix products, gradient(): jnp.einsum('yik,ikh->hy', col_factors, returned, preferred_element_type=j...  5.85 us
  transfers between devices with their start and end apart: 6, of which 6 were waited for; matrix products, arithmetic and copies ran while one was open for 0% of the time, Pallas kernels for 0%

profile of v1, /device:TPU:0, one launch (start us, length us, event | category | flops | bytes accessed | tf_op | source)
XLA Modules:
  0.0 172.1 jit_solution(13073980350378877076)
XLA Ops:
  0.6 0.0 copy-start
  0.7 0.7 copy-done
  1.3 0.2 dynamic-slice_reduce_fusion
  1.5 2.1 %copy.23 = bf16[512,16,128]{2,0,1:T(8,128)(2,1)S(1)} copy(bf16[512,16,128]{2,1,0:T(8,128)(2,1)} %param.13) | data formatting | bytes 4194304
  3.7 0.0 copy-start.7
  3.7 0.0 copy-start.3
  3.7 0.0 copy-start.6
  3.7 0.0 copy-start.8
  3.7 0.0 copy-start.9
  3.7 4.4 %copy.24 = bf16[512,16,128]{0,2,1:T(8,128)(2,1)} copy(bf16[512,16,128]{2,1,0:T(8,128)(2,1)} %param.12) | data formatting | bytes 4194304
  8.1 0.0 copy-done.3
  8.1 0.0 copy-done.6
  8.2 0.0 copy-start.4
  8.2 138.8 %while.23 = (s32[]{:T(128)}, f32[128,512]{1,0:T(8,128)S(1)}, f32[128,512]{1,0:T(8,128)S(1)}, f32[128]{0:T(128)S(1)}, f32[128]{0:T(128)S(1)}, /*index=5*/f32[128,...) while((s32[]{:T(128)}, f32[128,512]{1,0:T(8,128)S(1)}, ...), condition=%wide.region_4.5_spmd.clone, body=%wide.region_0.4_spmd.clone.sunk | while | flops 1080828416 | bytes 28880336 | solution.py:80
  8.2 0.1 convert_bitcast_fusion.4
  8.3 0.9 fusion.47
  9.2 22.7 %all_to_all.30 = bf16[32,64,128]{2,1,0:T(8,128)(2,1)S(1)} all-to-all(bf16[32,64,128]{2,1,0:T(8,128)(2,1)S(1)} %bitcast.77), channel_id=1, replica_groups=mesh['col'=8,'row'=4] {'col','row'}, dimensions={0} | all-to-all | bytes 1048576 | tf_op jit(solution)/shard_map/while/body/eval_jaxpr/all_to_all | solution.py:31
  31.9 0.1 bitcast_reduce_fusion.4
  32.0 0.1 collective-permute-start
  32.1 0.1 convert_bitcast_fusion.5
  32.1 1.4 collective-permute-done
  33.6 0.5 fusion.48
  34.1 0.7 fusion.49
  34.8 0.3 multiply_convert_fusion.2
  35.1 18.4 %all_to_all.31 = bf16[32,64,128]{2,1,0:T(8,128)(2,1)S(1)} all-to-all(bf16[32,64,128]{2,1,0:T(8,128)(2,1)S(1)} %bitcast.76), channel_id=1, replica_groups=mesh['col'=8,'row'=4] {'col','row'}, dimensions={0} | all-to-all | bytes 1048576 | tf_op jit(solution)/shard_map/while/body/eval_jaxpr/all_to_all | solution.py:31
  53.5 0.1 bitcast_reduce_fusion.5
  53.6 0.1 collective-permute-start.1
  53.7 1.6 collective-permute-done.1
  55.4 2.0 %fusion.50 = (f32[128]{0:T(128)S(1)}, f32[128,512]{1,0:T(8,128)S(1)}, f32[128,512]{1,0:T(8,128)S(1)}) fusion(f32[128,512]{1,0:T(8,128)S(1)} %get-tuple-element.580, f32[128,512]{1,0:T(8,128)S(1)} %fusion.48, f32[512]{0:T(512)S(1)} %bitcast.80, f32[128]{0:T(128)S(1)} %bitcast.82, pred[]{:T(512)S(6)} %lt.137, f32[128,512]{1,0:T(8,128)S(1)} %get-tuple-element.581, ...), kind=kOutput, calls=%fused_computation.29.clone.1 | convolution fusion | flops 271581056 | bytes 3935746 | tf_op jit(solution)/shard_map/while/body/eval_jaxpr/yik,ikh->hy/dot_general | solution.py:60
  57.4 0.1 convert_bitcast_fusion.4
  57.4 0.9 fusion.47
  58.3 18.4 %all_to_all.30 = bf16[32,64,128]{2,1,0:T(8,128)(2,1)S(1)} all-to-all(bf16[32,64,128]{2,1,0:T(8,128)(2,1)S(1)} %bitcast.77), channel_id=1, replica_groups=mesh['col'=8,'row'=4] {'col','row'}, dimensions={0} | all-to-all | bytes 1048576 | tf_op jit(solution)/shard_map/while/body/eval_jaxpr/all_to_all | solution.py:31
  76.7 0.1 bitcast_reduce_fusion.4
  76.8 0.1 collective-permute-start
  76.9 0.1 convert_bitcast_fusion.5
  77.0 1.4 collective-permute-done
  78.4 0.5 fusion.48
  78.9 0.7 fusion.49
  79.6 0.3 multiply_convert_fusion.2
  80.0 18.4 %all_to_all.31 = bf16[32,64,128]{2,1,0:T(8,128)(2,1)S(1)} all-to-all(bf16[32,64,128]{2,1,0:T(8,128)(2,1)S(1)} %bitcast.76), channel_id=1, replica_groups=mesh['col'=8,'row'=4] {'col','row'}, dimensions={0} | all-to-all | bytes 1048576 | tf_op jit(solution)/shard_map/while/body/eval_jaxpr/all_to_all | solution.py:31
  98.4 0.1 bitcast_reduce_fusion.5
  98.4 0.1 collective-permute-start.1
  98.5 1.6 collective-permute-done.1
  100.2 1.9 %fusion.50 = (f32[128]{0:T(128)S(1)}, f32[128,512]{1,0:T(8,128)S(1)}, f32[128,512]{1,0:T(8,128)S(1)}) fusion(f32[128,512]{1,0:T(8,128)S(1)} %get-tuple-element.580, f32[128,512]{1,0:T(8,128)S(1)} %fusion.48, f32[512]{0:T(512)S(1)} %bitcast.80, f32[128]{0:T(128)S(1)} %bitcast.82, pred[]{:T(512)S(6)} %lt.137, f32[128,512]{1,0:T(8,128)S(1)} %get-tuple-element.581, ...), kind=kOutput, calls=%fused_computation.29.clone.1 | convolution fusion | flops 271581056 | bytes 3935746 | tf_op jit(solution)/shard_map/while/body/eval_jaxpr/yik,ikh->hy/dot_general | solution.py:60
  102.2 0.1 convert_bitcast_fusion.4
  102.2 0.9 fusion.47
  103.2 18.4 %all_to_all.30 = bf16[32,64,128]{2,1,0:T(8,128)(2,1)S(1)} all-to-all(bf16[32,64,128]{2,1,0:T(8,128)(2,1)S(1)} %bitcast.77), channel_id=1, replica_groups=mesh['col'=8,'row'=4] {'col','row'}, dimensions={0} | all-to-all | bytes 1048576 | tf_op jit(solution)/shard_map/while/body/eval_jaxpr/all_to_all | solution.py:31
  121.6 0.1 bitcast_reduce_fusion.4
  121.6 0.1 collective-permute-start
  121.7 0.1 convert_bitcast_fusion.5
  121.8 1.4 collective-permute-done
  123.2 0.5 fusion.48
  123.7 0.7 fusion.49
  124.4 0.3 multiply_convert_fusion.2
  124.8 18.4 %all_to_all.31 = bf16[32,64,128]{2,1,0:T(8,128)(2,1)S(1)} all-to-all(bf16[32,64,128]{2,1,0:T(8,128)(2,1)S(1)} %bitcast.76), channel_id=1, replica_groups=mesh['col'=8,'row'=4] {'col','row'}, dimensions={0} | all-to-all | bytes 1048576 | tf_op jit(solution)/shard_map/while/body/eval_jaxpr/all_to_all | solution.py:31
  143.2 0.1 bitcast_reduce_fusion.5
  143.3 0.1 collective-permute-start.1
  143.4 1.6 collective-permute-done.1
  145.0 2.0 %fusion.50 = (f32[128]{0:T(128)S(1)}, f32[128,512]{1,0:T(8,128)S(1)}, f32[128,512]{1,0:T(8,128)S(1)}) fusion(f32[128,512]{1,0:T(8,128)S(1)} %get-tuple-element.580, f32[128,512]{1,0:T(8,128)S(1)} %fusion.48, f32[512]{0:T(512)S(1)} %bitcast.80, f32[128]{0:T(128)S(1)} %bitcast.82, pred[]{:T(512)S(6)} %lt.137, f32[128,512]{1,0:T(8,128)S(1)} %get-tuple-element.581, ...), kind=kOutput, calls=%fused_computation.29.clone.1 | convolution fusion | flops 271581056 | bytes 3935746 | tf_op jit(solution)/shard_map/while/body/eval_jaxpr/yik,ikh->hy/dot_general | solution.py:60
  147.0 0.0 copy-start.2
  147.0 0.0 copy-start.5
  147.0 0.1 subtract_reduce_fusion
  147.1 18.8 %psum.14 = f32[128]{0:T(128)S(1)} all-reduce(f32[128]{0:T(128)S(1)} %multiply_add_fusion), channel_id=1, replica_groups=mesh['col'=8,'row'=4] {'col'}, use_global_device_ids=true, to_apply=%region_6.7 | all-reduce | flops 128 | bytes 1024 | tf_op jit(solution)/shard_map/psum | solution.py:84
  166.0 6.2 %psum.15 = f32[128]{0:T(128)} all-reduce(f32[128]{0:T(128)S(1)} %psum.14), channel_id=1, replica_groups=mesh['col'=8,'row'=4] {'row'}, use_global_device_ids=true, to_apply=%region_7.8 | all-reduce | flops 128 | bytes 1024 | tf_op jit(solution)/shard_map/psum | solution.py:84
  (23 shorter events, 0.1 us)
Async XLA Ops:
  0.6 0.7 copy-start
  3.7 4.4 %copy-start.7 = (s32[512]{0:T(512)S(1)}, s32[512]{0:T(512)}, u32[]{:S(2)}) copy-start(s32[512]{0:T(512)} %param.16) | copy-start | bytes 6148
  3.7 4.4 %copy-start.3 = (f32[128,512]{1,0:T(8,128)S(1)}, f32[128,512]{1,0:T(8,128)}, u32[]{:S(2)}) copy-start(f32[128,512]{1,0:T(8,128)} %param.10) | copy-start | bytes 786436
  3.7 4.4 %copy-start.6 = (f32[128,512]{1,0:T(8,128)S(1)}, f32[128,512]{1,0:T(8,128)}, u32[]{:S(2)}) copy-start(f32[128,512]{1,0:T(8,128)} %param.11) | copy-start | bytes 786436
  3.7 4.4 %copy-start.8 = (f32[512]{0:T(512)S(1)}, f32[512]{0:T(512)}, u32[]{:S(2)}) copy-start(f32[512]{0:T(512)} %param.15) | copy-start | bytes 6148
  3.7 4.4 %copy-start.9 = (f32[128]{0:T(128)S(1)}, f32[128]{0:T(128)}, u32[]{:S(2)}) copy-start(f32[128]{0:T(128)} %param.17) | copy-start | bytes 1540
  8.2 138.9 %copy-start.4 = (f32[128,512]{1,0:T(8,128)S(1)}, f32[128,512]{1,0:T(8,128)}, u32[]{:S(2)}) copy-start(f32[128,512]{1,0:T(8,128)} %param.11) | copy-start | bytes 786436
  8.3 25.4 %copy-start.1 = (bf16[512,16,128]{0,2,1:T(8,128)(2,1)S(1)}, bf16[512,16,128]{0,2,1:T(8,128)(2,1)}, u32[]{:S(2)}) copy-start(bf16[512,16,128]{0,2,1:T(8,128)(2,1)} %get-tuple-element.607) | copy-start | bytes 6291460 | tf_op jit(solution)/shard_map/while
  32.0 1.6 collective-permute-start
  53.6 1.7 %collective-permute-start.1 = (bf16[16,64,128]{2,1,0:T(8,128)(2,1)S(1)}, bf16[16,64,128]{2,1,0:T(8,128)(2,1)}, u32[]{:S(2)}, u32[]{:S(2)}) collective-permute-start(bf16[16,64,128]{2,1,0:T(8,128)(2,1)S(1)} %bitcast_reduce_fusion.5), channel_id=1, source_target_pairs={{0,1},{1,0},{2,3},{3,2},{4,5},{5,4},{6,7},{7,6},{8,9},{9,8},{10,11... | collective-permute-start | bytes 786440 | tf_op jit(solution)/shard_map/while/body/eval_jaxpr/ppermute | solution.py:10
  57.4 21.0 %copy-start.1 = (bf16[512,16,128]{0,2,1:T(8,128)(2,1)S(1)}, bf16[512,16,128]{0,2,1:T(8,128)(2,1)}, u32[]{:S(2)}) copy-start(bf16[512,16,128]{0,2,1:T(8,128)(2,1)} %get-tuple-element.607) | copy-start | bytes 6291460 | tf_op jit(solution)/shard_map/while
  76.8 1.6 collective-permute-start
  98.4 1.7 %collective-permute-start.1 = (bf16[16,64,128]{2,1,0:T(8,128)(2,1)S(1)}, bf16[16,64,128]{2,1,0:T(8,128)(2,1)}, u32[]{:S(2)}, u32[]{:S(2)}) collective-permute-start(bf16[16,64,128]{2,1,0:T(8,128)(2,1)S(1)} %bitcast_reduce_fusion.5), channel_id=1, source_target_pairs={{0,1},{1,0},{2,3},{3,2},{4,5},{5,4},{6,7},{7,6},{8,9},{9,8},{10,11... | collective-permute-start | bytes 786440 | tf_op jit(solution)/shard_map/while/body/eval_jaxpr/ppermute | solution.py:10
  102.2 21.0 %copy-start.1 = (bf16[512,16,128]{0,2,1:T(8,128)(2,1)S(1)}, bf16[512,16,128]{0,2,1:T(8,128)(2,1)}, u32[]{:S(2)}) copy-start(bf16[512,16,128]{0,2,1:T(8,128)(2,1)} %get-tuple-element.607) | copy-start | bytes 6291460 | tf_op jit(solution)/shard_map/while
  121.6 1.6 collective-permute-start
  143.3 1.7 %collective-permute-start.1 = (bf16[16,64,128]{2,1,0:T(8,128)(2,1)S(1)}, bf16[16,64,128]{2,1,0:T(8,128)(2,1)}, u32[]{:S(2)}, u32[]{:S(2)}) collective-permute-start(bf16[16,64,128]{2,1,0:T(8,128)(2,1)S(1)} %bitcast_reduce_fusion.5), channel_id=1, source_target_pairs={{0,1},{1,0},{2,3},{3,2},{4,5},{5,4},{6,7},{7,6},{8,9},{9,8},{10,11... | collective-permute-start | bytes 786440 | tf_op jit(solution)/shard_map/while/body/eval_jaxpr/ppermute | solution.py:10
  147.0 25.1 %copy-start.2 = (f32[128,512]{1,0:T(8,128)}, f32[128,512]{1,0:T(8,128)S(1)}, u32[]{:S(2)}) copy-start(f32[128,512]{1,0:T(8,128)S(1)} %get-tuple-element.347) | copy-start | bytes 786436
  147.0 25.1 %copy-start.5 = (f32[128,512]{1,0:T(8,128)}, f32[128,512]{1,0:T(8,128)S(1)}, u32[]{:S(2)}) copy-start(f32[128,512]{1,0:T(8,128)S(1)} %get-tuple-element.348) | copy-start | bytes 786436
